TPU v7x, 512 devices: a whole 4x8x8 slice. The times are simulated.
512 devices in a mesh: loop: 32 (over z, x_hi, core), rep: 16 (over x_lo, y).
Axes of the slice: x: 4 (x_hi: 2, x_lo: 2; x = x_hi * 2 + x_lo), y: 8, z: 8, core: 2. Of those that a mesh axis runs over, the one named last changes fastest.
Arguments:
- lam: bfloat16 [8, 384, 16384], P(None, None, ('rep', 'loop')), may hold values from -6 to 6
- integrals: bfloat16 [8, 16384, 8192], P(None, 'rep', 'loop'), may hold values from -0.046875 to 0.046875
- block_mask: int32 [8, 512], P(None, 'rep'), may hold values 0 or 1
Outputs:
- ladder: bfloat16 [8, 384, 8192], P(None, 'rep', 'loop')
All inputs are finite; a program needn't handle non-finite values. No bound on the sum of `block_mask` on one device may be relied on, other than what follows from the above.
Results may differ from a plain program's by a relative error of at most 0.001.
Values may be sent and summed in bfloat16 or wider, within the bound.
A program may use at most 64 MiB of HBM per device.

v0:
```python
import jax
import jax.numpy as jnp
from jax import lax
from jax.sharding import PartitionSpec as P


def per_device(lam, integrals, block_mask):
    block_rows = lam.shape[2]
    live = jnp.repeat(block_mask, block_rows, axis=1) == 1
    kept = jnp.where(live[:, :, None], integrals, jnp.zeros_like(integrals))
    layer_lam = lax.all_gather(lam, "loop", axis=2, tiled=True)
    partial_sum = jnp.einsum("hpk,hka->hpa", layer_lam, kept, preferred_element_type=jnp.float32)
    own_rows = lam.shape[1] // lax.axis_size("rep")
    summed = lax.psum(partial_sum, "rep")
    result = lax.dynamic_slice_in_dim(summed, lax.axis_index("rep") * own_rows, own_rows, 1)
    return result.astype(jnp.bfloat16)


def solution(mesh):
    return jax.shard_map(
        per_device,
        mesh=mesh,
        in_specs=(P(None, None, ("rep", "loop")), P(None, "rep", "loop"), P(None, "rep")),
        out_specs=P(None, "rep", "loop"),
        check_vma=False,
    )
```

profile of v0, /device:TPU:2, one launch (start us, length us, event | category | flops | bytes accessed | tf_op | source)
XLA Modules:
  0.0 214.6 jit_solution(9378206636416580272)
XLA Ops:
  6.5 0.0 all-gather.2.cloned.1.call-start
  6.5 0.7 all-gather.2.cloned.1.call-update
  7.3 0.7 broadcast_compare_fusion
  8.0 0.1 broadcast_in_dim.15
  8.1 0.1 eq.16
  8.2 106.1 %all-gather.2.cloned.1.call-done = bf16[8,384,1024]{1,2,0:T(8,128)(2,1)} async-done(((bf16[8,384,32]{1,2,0:T(8,128)(2,1)}), bf16[8,384,1024]{1,2,0:T(8,128)(2,1)}) %all-gather.2.cloned.1.call-update) | async-done | bytes 6291472 | tf_op jit(solution)/shard_map/all_gather | solution.py:11
  114.3 6.1 %fusion.4 = f32[8,384,256]{2,1,0:T(8,128)S(1)} fusion(bf16[8,384,1024]{1,2,0:T(8,128)(2,1)} %all-gather.2.cloned.1.call-done, bf16[8,1024,256]{2,1,0:T(8,128)(2,1)} %param.4, pred[8,1024]{1,0:T(8,128)(4,1)S(1)} %eq.16), kind=kOutput, calls=%fused_computation.4 | convolution fusion | flops 1612709888 | bytes 13639680 | tf_op jit(solution)/shard_map/hpk,hka->hpa/dot_general | solution.py:12
  120.5 85.7 %all-reduce.1 = bf16[8,384,256]{2,1,0:T(8,128)(2,1)} all-reduce(f32[8,384,256]{2,1,0:T(8,128)S(1)} %fusion.4), channel_id=1, replica_groups=mesh['loop'=32,'rep'=16] {'rep'}, use_global_device_ids=true, to_apply=%region_0.1 | all-reduce | flops 786432 | bytes 4718592 | tf_op jit(solution)/shard_map/psum | solution.py:14
  206.2 1.5 dynamic-slice_convert_fusion
Async XLA Ops:
  6.5 107.8 %all-gather.2.cloned.1.call-start = ((), (), s32[]{:S(2)}) async-start(), calls=%async_computation | async-start | bytes 6488064 | tf_op jit(solution)/shard_map/all_gather | solution.py:11
Sparse Core Ops, SparseCore 0:
  10.6 103.6 all-gather.1
where the time goes:
time: 215 us
  waiting for transfers between devices  107 us (50%)
  blocking collectives  85.7 us (40%)
  between operations  13.4 us (6%)
  matrix products  6.13 us (3%)
    all_gather x1, waiting for transfers between devices, per_device(): layer_lam = lax.all_gather(lam, 'loop', axis=2, tiled=True)  106 us
    psum x1, blocking collectives, per_device(): summed = lax.psum(partial_sum, 'rep')  85.7 us
    dot_general x1, matrix products, per_device(): jnp.einsum('hpk,hka->hpa', layer_lam, kept, preferred_element_type=jnp.fl...  6.13 us
  transfers between devices with their start and end apart: 1, of which 1 were waited for; matrix products, arithmetic and copies ran while one was open for 0% of the time, Pallas kernels for 0%

commit v1 on v0

v1 whole, which is shorter than its diff:
```python
import functools

import jax
import jax.numpy as jnp
from jax import lax
from jax.experimental import pallas as pl
from jax.experimental.pallas import tpu as pltpu
from jax.sharding import PartitionSpec as P

MESH = pl.DeviceIdType.MESH
NZ = 8
NY = 8
NQ = 4
F32 = jnp.float32


def kernel(nh, lam, w, mask, out, q_buf, a_buf, w_buf, p_buf, r_buf, x_buf, fx_buf, t_buf, s_buf,
           lam_s, lam_r, lam_l, w_s, w_r, w_l, ag_s, ag_r, rs_s, rs_r, x_s, x_r, t_s, t_r):
    nst = 2 * nh
    ij = lam.shape[2]
    half = ij // 2
    ab = w.shape[2]
    rows = half // NY

    loop = lax.axis_index("loop")
    rep = lax.axis_index("rep")
    z = loop // NQ
    quad = loop % NQ
    core = loop % 2
    x_hi = quad // 2
    x_lo = rep // NY
    y = rep % NY
    first = core * nh
    other = (1 - core) * nh

    def dev(loop_to, rep_to):
        return {"loop": loop_to, "rep": rep_to}

    sibling = dev(z * NQ + x_hi * 2 + (1 - core), rep)
    quads = (
        (sibling, other),
        (dev(z * NQ + (1 - x_hi) * 2 + core, rep), first),
        (dev(z * NQ + (1 - x_hi) * 2 + (1 - core), rep), other),
    )
    z_to = (dev((z + 1) % NZ * NQ + quad, rep), dev((z + NZ - 1) % NZ * NQ + quad, rep))
    y_to = (dev(loop, x_lo * NY + (y + 1) % NY), dev(loop, x_lo * NY + (y + NY - 1) % NY))
    x_to = dev(loop, (1 - x_lo) * NY + y)

    def remote(src, dst, send, recv, to):
        return pltpu.make_async_remote_copy(
            src_ref=src, dst_ref=dst, send_sem=send, recv_sem=recv, device_id=to, device_id_type=MESH)

    def lam_local(i):
        return pltpu.make_async_copy(lam.at[first + i], q_buf.at[i, quad], lam_l.at[i])

    def w_local(i):
        return pltpu.make_async_copy(w.at[first + i], w_buf.at[0, i], w_l.at[i])

    for i in range(nh):
        lam_local(i).start()
    for i in range(nh):
        w_local(i).start()

    barrier = pltpu.get_barrier_semaphore()
    peers = [to for to, _ in quads] + list(z_to) + list(y_to) + [x_to]
    for to in peers:
        pl.semaphore_signal(barrier, inc=1, device_id=to, device_id_type=MESH)
    pl.semaphore_wait(barrier, len(peers))

    def lam_send(d, i):
        to, h0 = quads[d]
        return remote(lam.at[h0 + i], q_buf.at[i, quad], lam_s.at[d, i], lam_r.at[d, i], to)

    def w_send(i):
        return remote(w.at[other + i], w_buf.at[1, i], w_s.at[i], w_r.at[i], sibling)

    for i in range(nh):
        for d in (1, 2, 0):
            lam_send(d, i).start()
    for i in range(nh):
        w_send(i).start()

    def prep(i):
        lam_local(i).wait()
        for d in range(3):
            lam_send(d, i).wait_recv()
        parts = []
        for k in range(NQ):
            live = mask[first + i, z * NQ + k].astype(F32)
            parts.append(q_buf[i, k].astype(F32) * live)
        block = jnp.concatenate(parts, axis=0).T.astype(jnp.bfloat16)
        a_buf[2 * i + (1 - x_lo), z] = block[:half]
        a_buf[2 * i + x_lo, z] = block[half:]

    def ag_hops(d, s):
        return NZ // 2 if d == s % 2 else NZ // 2 - 1

    def ag_from(d, back):
        return (z + NZ - back) % NZ if d == 0 else (z + back) % NZ

    def ag_copy(d, s, k, back):
        block = a_buf.at[s, ag_from(d, back)]
        return remote(block, block, ag_s.at[d, s, k - 1], ag_r.at[d, s, k - 1], z_to[d])

    def ag_start(d, s, k):
        ag_copy(d, s, k, k - 1).start()

    def ag_wait(d, s, k):
        ag_copy(d, s, k, k).wait_recv()

    def rs_hops(d, s):
        return NY // 2 if d == s % 2 else NY // 2 - 1

    def rs_owner(d, m):
        return (y + m) % NY if d == 0 else (y + NY - m) % NY

    def rs_copy(d, s, m):
        src = p_buf.at[s, rs_owner(d, m)] if m == rs_hops(d, s) else r_buf.at[d, s, m]
        return remote(src, r_buf.at[d, s, m - 1], rs_s.at[d, s, m - 1], rs_r.at[d, s, m - 1], y_to[d])

    def rs_arrive(d, s, m):
        rs_copy(d, s, m + 1).wait_recv()
        if m > 0:
            r_buf[d, s, m] = r_buf[d, s, m] + p_buf[s, rs_owner(d, m)]
            rs_copy(d, s, m).start()

    def x_copy(i):
        return remote(fx_buf.at[i], x_buf.at[i], x_s.at[i], x_r.at[i], x_to)

    def t_copy(i):
        return remote(t_buf.at[i], s_buf.at[i], t_s.at[i], t_r.at[i], sibling)

    def matmul(s):
        i = s // 2
        if s % 2 == 0:
            w_local(i).wait()
            w_send(i).wait_recv()
        block = jnp.concatenate([a_buf[s, k] for k in range(NZ)], axis=1)
        for side in range(2):
            part = jnp.dot(block, w_buf[side, i], preferred_element_type=F32)
            p_buf[s, :, :, side * ab:(side + 1) * ab] = part.reshape(NY, rows, ab)

    def final(s):
        i = s // 2
        total = p_buf[s, y] + r_buf[0, s, 0] + r_buf[1, s, 0]
        if s % 2 == 0:
            fx_buf[i] = total
            x_copy(i).start()
        else:
            x_copy(i).wait_recv()
            done = (total + x_buf[i]).astype(jnp.bfloat16)
            out[first + i] = done[:, :ab]
            t_buf[i] = done[:, ab:]
            t_copy(i).start()

    def phase(s, p):
        if p == 0:
            if s % 2 == 0:
                prep(s // 2)
            for d in range(2):
                ag_start(d, s, 1)
        elif p <= 4:
            for d in range(2):
                if p <= ag_hops(d, s):
                    ag_wait(d, s, p)
                    if p < ag_hops(d, s):
                        ag_start(d, s, p + 1)
            if p == 4:
                matmul(s)
                for d in range(2):
                    rs_copy(d, s, rs_hops(d, s)).start()
        else:
            for d in range(2):
                m = rs_hops(d, s) - (p - 4)
                if m >= 0:
                    rs_arrive(d, s, m)
            if p == 8:
                final(s)

    for tick in range(nst + 8):
        for p in (3, 7, 2, 6, 1, 5, 0, 4, 8):
            if 0 <= tick - p < nst:
                phase(tick - p, p)

    for i in range(nh):
        t_copy(i).wait_recv()
        out[other + i] = s_buf[i]

    for i in range(nh):
        for d in range(3):
            lam_send(d, i).wait_send()
        w_send(i).wait_send()
        x_copy(i).wait_send()
        t_copy(i).wait_send()
    for s in range(nst):
        for d in range(2):
            for k in range(1, ag_hops(d, s) + 1):
                ag_copy(d, s, k, k - 1).wait_send()
            for m in range(1, rs_hops(d, s) + 1):
                rs_copy(d, s, m).wait_send()


def per_device(lam, integrals, block_mask):
    nirrep, ij, cb = lam.shape
    _, cd, ab = integrals.shape
    nh = nirrep // 2
    nst = 2 * nh
    half = ij // 2
    rows = half // NY
    bf = jnp.bfloat16
    dma = pltpu.SemaphoreType.DMA
    any_spec = pl.BlockSpec(memory_space=pl.ANY)
    return pl.pallas_call(
        functools.partial(kernel, nh),
        out_shape=jax.ShapeDtypeStruct((nirrep, rows, ab), bf),
        in_specs=[any_spec, any_spec, pl.BlockSpec(memory_space=pltpu.SMEM)],
        out_specs=pl.BlockSpec(memory_space=pltpu.VMEM),
        scratch_shapes=[
            pltpu.VMEM((nh, NQ, cb, ij), bf),
            pltpu.VMEM((nst, NZ, half, NQ * cb), bf),
            pltpu.VMEM((2, nh, cd, ab), bf),
            pltpu.VMEM((nst, NY, rows, 2 * ab), F32),
            pltpu.VMEM((2, nst, 4, rows, 2 * ab), F32),
            pltpu.VMEM((nh, rows, 2 * ab), F32),
            pltpu.VMEM((nh, rows, 2 * ab), F32),
            pltpu.VMEM((nh, rows, ab), bf),
            pltpu.VMEM((nh, rows, ab), bf),
            dma((3, nh)), dma((3, nh)), dma((nh,)),
            dma((nh,)), dma((nh,)), dma((nh,)),
            dma((2, nst, 4)), dma((2, nst, 4)),
            dma((2, nst, 4)), dma((2, nst, 4)),
            dma((nh,)), dma((nh,)),
            dma((nh,)), dma((nh,)),
        ],
        compiler_params=pltpu.CompilerParams(collective_id=0, has_side_effects=True),
    )(lam.transpose(0, 2, 1), integrals, block_mask)


def solution(mesh):
    return jax.shard_map(
        per_device,
        mesh=mesh,
        in_specs=(P(None, None, ("rep", "loop")), P(None, "rep", "loop"), P(None, "rep")),
        out_specs=P(None, "rep", "loop"),
        check_vma=False,
    )
```

time: 215 us -> 91.1 us (0.42)
  the two profiles are of different devices: /device:TPU:2 before, /device:TPU:1 now
where the time goes in v1:
time: 91.1 us; the launch traced here: 90.8 us
  Pallas kernels  89.2 us (98%)
  local copies, waits for them, and re-layouts  1.54 us (2%)
    pallas_call x1, Pallas kernels, per_device(): pl.pallas_call(functools.partial(kernel, nh), out_shape=jax.ShapeDtypeStr...  89.2 us

profile of v1, /device:TPU:1, one launch (start us, length us, event | category | flops | bytes accessed | tf_op | source)
XLA Modules:
  0.0 90.8 jit_solution(7676405313947508542)
XLA Ops:
  0.0 89.2 %shard_map.37 = bf16[8,24,256]{2,1,0:T(8,128)(2,1)} custom-call(bf16[8,32,384]{2,1,0:T(8,128)(2,1)} %bitcast.1, bf16[8,1024,256]{2,1,0:T(8,128)(2,1)} %w.1, s32[8,32]{1,0:T(8,128)} %mask.1), custom_call_target="tpu_custom_call" | custom-call | tf_op jit(solution)/shard_map/pallas_call | solution.py:213
  89.2 1.5 %copy.5 = bf16[8,24,256]{2,1,0:T(8,128)(2,1)} copy(bf16[8,24,256]{2,1,0:T(8,128)(2,1)} %shard_map.37) | data formatting | bytes 196608

commit v2 on v1

--- a/solution.py
+++ b/solution.py
@@ -12,9 +12,25 @@
 NY = 8
 NQ = 4
 F32 = jnp.float32
-
-
-def kernel(nh, lam, w, mask, out, q_buf, a_buf, w_buf, p_buf, r_buf, x_buf, fx_buf, t_buf, s_buf,
+I16 = jnp.int16
+SCALE_ROWS = 16
+
+
+def encode(v):
+    top = jnp.maximum(jnp.max(jnp.abs(v), axis=0, keepdims=True), 1e-37)
+    c = jnp.maximum(jnp.ceil(jnp.log2(top)) - 15, -126)
+    q = jnp.clip(jnp.round(v * jnp.exp2(-c)), -32767, 32767)
+    coded = jnp.concatenate([q, jnp.broadcast_to(c, (SCALE_ROWS, v.shape[1]))], axis=0)
+    return coded.astype(jnp.int32).astype(I16)
+
+
+def decode(coded):
+    f = coded.astype(jnp.int32).astype(F32)
+    rows = f.shape[0] - SCALE_ROWS
+    return f[:rows] * jnp.exp2(f[rows:rows + 1])
+
+
+def kernel(nh, lam, w, mask, out, q_buf, a_buf, w_buf, p_buf, e_buf, r_buf, x_buf, fx_buf, t_buf, s_buf,
            lam_s, lam_r, lam_l, w_s, w_r, w_l, ag_s, ag_r, rs_s, rs_r, x_s, x_r, t_s, t_r):
     nst = 2 * nh
     ij = lam.shape[2]
@@ -115,13 +131,17 @@
         return (y + m) % NY if d == 0 else (y + NY - m) % NY
 
     def rs_copy(d, s, m):
-        src = p_buf.at[s, rs_owner(d, m)] if m == rs_hops(d, s) else r_buf.at[d, s, m]
-        return remote(src, r_buf.at[d, s, m - 1], rs_s.at[d, s, m - 1], rs_r.at[d, s, m - 1], y_to[d])
+        return remote(e_buf.at[d, s, m - 1], r_buf.at[d, s, m - 1], rs_s.at[d, s, m - 1], rs_r.at[d, s, m - 1], y_to[d])
+
+    def rs_start(d, s):
+        m = rs_hops(d, s)
+        e_buf[d, s, m - 1] = encode(p_buf[s, rs_owner(d, m)])
+        rs_copy(d, s, m).start()
 
     def rs_arrive(d, s, m):
         rs_copy(d, s, m + 1).wait_recv()
         if m > 0:
-            r_buf[d, s, m] = r_buf[d, s, m] + p_buf[s, rs_owner(d, m)]
+            e_buf[d, s, m - 1] = encode(decode(r_buf[d, s, m]) + p_buf[s, rs_owner(d, m)])
             rs_copy(d, s, m).start()
 
     def x_copy(i):
@@ -138,19 +158,19 @@
         block = jnp.concatenate([a_buf[s, k] for k in range(NZ)], axis=1)
         for side in range(2):
             part = jnp.dot(block, w_buf[side, i], preferred_element_type=F32)
-            p_buf[s, :, :, side * ab:(side + 1) * ab] = part.reshape(NY, rows, ab)
+            p_buf[s, :, side * rows:(side + 1) * rows] = part.reshape(NY, rows, ab)
 
     def final(s):
         i = s // 2
-        total = p_buf[s, y] + r_buf[0, s, 0] + r_buf[1, s, 0]
+        total = p_buf[s, y] + decode(r_buf[0, s, 0]) + decode(r_buf[1, s, 0])
         if s % 2 == 0:
             fx_buf[i] = total
             x_copy(i).start()
         else:
             x_copy(i).wait_recv()
             done = (total + x_buf[i]).astype(jnp.bfloat16)
-            out[first + i] = done[:, :ab]
-            t_buf[i] = done[:, ab:]
+            out[first + i] = done[:rows]
+            t_buf[i] = done[rows:]
             t_copy(i).start()
 
     def phase(s, p):
@@ -168,7 +188,7 @@
             if p == 4:
                 matmul(s)
                 for d in range(2):
-                    rs_copy(d, s, rs_hops(d, s)).start()
+                    rs_start(d, s)
         else:
             for d in range(2):
                 m = rs_hops(d, s) - (p - 4)
@@ -219,10 +239,11 @@
             pltpu.VMEM((nh, NQ, cb, ij), bf),
             pltpu.VMEM((nst, NZ, half, NQ * cb), bf),
             pltpu.VMEM((2, nh, cd, ab), bf),
-            pltpu.VMEM((nst, NY, rows, 2 * ab), F32),
-            pltpu.VMEM((2, nst, 4, rows, 2 * ab), F32),
-            pltpu.VMEM((nh, rows, 2 * ab), F32),
-            pltpu.VMEM((nh, rows, 2 * ab), F32),
+            pltpu.VMEM((nst, NY, 2 * rows, ab), F32),
+            pltpu.VMEM((2, nst, 4, 2 * rows + SCALE_ROWS, ab), I16),
+            pltpu.VMEM((2, nst, 4, 2 * rows + SCALE_ROWS, ab), I16),
+            pltpu.VMEM((nh, 2 * rows, ab), F32),
+            pltpu.VMEM((nh, 2 * rows, ab), F32),
             pltpu.VMEM((nh, rows, ab), bf),
             pltpu.VMEM((nh, rows, ab), bf),
             dma((3, nh)), dma((3, nh)), dma((nh,)),

time: 91.1 us -> 88 us (0.966)
  Pallas kernels: 89.2 us -> 86.3 us
    pallas_call x1, Pallas kernels: 89.2 us -> 86.3 us  [per_device(): pl.pallas_call(functools.partial(kernel, nh), out_shape=jax.ShapeDtypeStr...]
where the time goes in v2:
time: 88 us; the launch traced here: 87.8 us
  Pallas kernels  86.3 us (98%)
  local copies, waits for them, and re-layouts  1.54 us (2%)
    pallas_call x1, Pallas kernels, per_device(): pl.pallas_call(functools.partial(kernel, nh), out_shape=jax.ShapeDtypeStr...  86.3 us

profile of v2, /device:TPU:1, one launch (start us, length us, event | category | flops | bytes accessed | tf_op | source)
XLA Modules:
  0.0 87.8 jit_solution(4082541579253113226)
XLA Ops:
  0.0 86.3 %shard_map.37 = bf16[8,24,256]{2,1,0:T(8,128)(2,1)} custom-call(bf16[8,32,384]{2,1,0:T(8,128)(2,1)} %bitcast.1, bf16[8,1024,256]{2,1,0:T(8,128)(2,1)} %w.1, s32[8,32]{1,0:T(8,128)} %mask.1), custom_call_target="tpu_custom_call" | custom-call | tf_op jit(solution)/shard_map/pallas_call | solution.py:233
  86.3 1.5 %copy.5 = bf16[8,24,256]{2,1,0:T(8,128)(2,1)} copy(bf16[8,24,256]{2,1,0:T(8,128)(2,1)} %shard_map.37) | data formatting | bytes 196608

commit v3 on v2

--- a/solution.py
+++ b/solution.py
@@ -14,6 +14,27 @@
 F32 = jnp.float32
 I16 = jnp.int16
 SCALE_ROWS = 16
+
+ORDER = (
+    (0, 0), (1, 0), (1, 1), (0, 1), (1, 2), (1, 3), (0, 2), (0, 3), (2, 0, 0, 1), (2, 1, 0, 1), (2, 0, 1, 1),
+    (2, 1, 1, 1), (2, 0, 2, 1), (2, 1, 2, 1), (2, 0, 3, 1), (2, 1, 3, 1), (2, 0, 0, 2), (2, 1, 0, 2),
+    (2, 0, 1, 2), (2, 1, 1, 2), (2, 0, 2, 2), (2, 1, 2, 2), (2, 0, 3, 2), (2, 1, 3, 2), (2, 0, 0, 3),
+    (2, 1, 0, 3), (1, 4), (2, 0, 1, 3), (2, 1, 1, 3), (1, 5), (2, 0, 2, 3), (2, 1, 2, 3), (1, 6),
+    (2, 0, 3, 3), (2, 1, 3, 3), (1, 7), (2, 1, 4, 1), (2, 0, 0, 4), (3, 0), (2, 1, 1, 4), (3, 1),
+    (2, 0, 4, 1), (2, 0, 5, 1), (2, 1, 5, 1), (2, 1, 6, 1), (2, 0, 2, 4), (3, 2), (4, 0, 0, 1), (4, 1, 0, 1),
+    (2, 0, 6, 1), (2, 1, 3, 4), (3, 3), (2, 0, 7, 1), (2, 1, 7, 1), (4, 0, 1, 1), (4, 1, 1, 1), (2, 0, 4, 2),
+    (2, 1, 4, 2), (4, 0, 2, 1), (4, 1, 2, 1), (2, 0, 5, 2), (2, 1, 5, 2), (4, 0, 0, 2), (4, 1, 0, 2),
+    (4, 0, 3, 1), (2, 0, 6, 2), (2, 1, 6, 2), (4, 1, 3, 1), (4, 0, 1, 2), (4, 1, 1, 2), (2, 0, 7, 2),
+    (2, 1, 7, 2), (4, 0, 2, 2), (4, 1, 2, 2), (2, 0, 4, 3), (2, 1, 4, 3), (4, 0, 0, 3), (4, 1, 0, 3),
+    (2, 0, 5, 3), (2, 1, 5, 3), (4, 0, 3, 2), (4, 1, 3, 2), (4, 0, 1, 3), (2, 0, 6, 3), (2, 1, 6, 3),
+    (4, 1, 1, 3), (4, 0, 2, 3), (4, 1, 2, 3), (2, 0, 7, 3), (2, 1, 7, 3), (4, 0, 0, 4), (5, 0), (2, 0, 4, 4),
+    (3, 4), (4, 0, 3, 3), (4, 1, 3, 3), (4, 1, 1, 4), (2, 0, 6, 4), (3, 6), (2, 1, 5, 4), (3, 5),
+    (2, 1, 7, 4), (3, 7), (4, 0, 4, 1), (4, 1, 4, 1), (4, 1, 3, 4), (5, 1), (4, 0, 6, 1), (4, 0, 2, 4),
+    (5, 2), (4, 1, 6, 1), (4, 0, 5, 1), (4, 1, 5, 1), (4, 0, 7, 1), (4, 1, 7, 1), (4, 0, 4, 2), (4, 1, 4, 2),
+    (4, 0, 6, 2), (4, 1, 6, 2), (5, 3), (4, 0, 5, 2), (4, 1, 5, 2), (4, 0, 7, 2), (4, 1, 7, 2), (4, 0, 4, 3),
+    (4, 1, 4, 3), (4, 0, 6, 3), (4, 1, 6, 3), (4, 0, 5, 3), (4, 1, 5, 3), (4, 0, 7, 3), (4, 1, 7, 3),
+    (4, 0, 4, 4), (5, 4), (4, 0, 6, 4), (5, 6), (4, 1, 5, 4), (4, 1, 7, 4), (5, 5), (5, 7),
+)
 
 
 def encode(v):
@@ -173,34 +194,26 @@
             t_buf[i] = done[rows:]
             t_copy(i).start()
 
-    def phase(s, p):
-        if p == 0:
-            if s % 2 == 0:
-                prep(s // 2)
-            for d in range(2):
-                ag_start(d, s, 1)
-        elif p <= 4:
-            for d in range(2):
-                if p <= ag_hops(d, s):
-                    ag_wait(d, s, p)
-                    if p < ag_hops(d, s):
-                        ag_start(d, s, p + 1)
-            if p == 4:
-                matmul(s)
-                for d in range(2):
-                    rs_start(d, s)
-        else:
-            for d in range(2):
-                m = rs_hops(d, s) - (p - 4)
-                if m >= 0:
-                    rs_arrive(d, s, m)
-            if p == 8:
-                final(s)
-
-    for tick in range(nst + 8):
-        for p in (3, 7, 2, 6, 1, 5, 0, 4, 8):
-            if 0 <= tick - p < nst:
-                phase(tick - p, p)
+    def gather_step(d, s, k):
+        ag_wait(d, s, k)
+        if k < ag_hops(d, s):
+            ag_start(d, s, k + 1)
+
+    def gather_first(s):
+        for d in range(2):
+            ag_start(d, s, 1)
+
+    def multiply(s):
+        matmul(s)
+        for d in range(2):
+            rs_start(d, s)
+
+    def sum_step(d, s, k):
+        rs_arrive(d, s, rs_hops(d, s) - k)
+
+    steps = (prep, gather_first, gather_step, multiply, sum_step, final)
+    for kind, *which in ORDER:
+        steps[kind](*which)
 
     for i in range(nh):
         t_copy(i).wait_recv()

time: 88 us -> 75.1 us (0.85)
  Pallas kernels: 86.3 us -> 73.3 us
    pallas_call x1, Pallas kernels: 86.3 us -> 73.3 us  [per_device(): pl.pallas_call(functools.partial(kernel, nh), out_shape=jax.ShapeDtypeStr...]
where the time goes in v3:
time: 75.1 us; the launch traced here: 74.9 us
  Pallas kernels  73.3 us (98%)
  local copies, waits for them, and re-layouts  1.54 us (2%)
    pallas_call x1, Pallas kernels, per_device(): pl.pallas_call(functools.partial(kernel, nh), out_shape=jax.ShapeDtypeStr...  73.3 us
    unnamed x1, local copies, waits for them, and re-layouts  1.54 us

profile of v3, /device:TPU:1, one launch (start us, length us, event | category | flops | bytes accessed | tf_op | source)
XLA Modules:
  0.0 74.9 jit_solution(13230241804063941113)
XLA Ops:
  0.0 73.3 %shard_map.37 = bf16[8,24,256]{2,1,0:T(8,128)(2,1)} custom-call(bf16[8,32,384]{2,1,0:T(8,128)(2,1)} %bitcast.1, bf16[8,1024,256]{2,1,0:T(8,128)(2,1)} %w.1, s32[8,32]{1,0:T(8,128)} %mask.1), custom_call_target="tpu_custom_call" | custom-call | tf_op jit(solution)/shard_map/pallas_call | solution.py:246
  73.3 1.5 %copy.5 = bf16[8,24,256]{2,1,0:T(8,128)(2,1)} copy(bf16[8,24,256]{2,1,0:T(8,128)(2,1)} %shard_map.37) | data formatting | bytes 196608

commit v4 on v3

--- a/solution.py
+++ b/solution.py
@@ -10,30 +10,29 @@
 MESH = pl.DeviceIdType.MESH
 NZ = 8
 NY = 8
+NF = 2
 NQ = 4
 F32 = jnp.float32
 I16 = jnp.int16
 SCALE_ROWS = 16
 
 ORDER = (
-    (0, 0), (1, 0), (1, 1), (0, 1), (1, 2), (1, 3), (0, 2), (0, 3), (2, 0, 0, 1), (2, 1, 0, 1), (2, 0, 1, 1),
-    (2, 1, 1, 1), (2, 0, 2, 1), (2, 1, 2, 1), (2, 0, 3, 1), (2, 1, 3, 1), (2, 0, 0, 2), (2, 1, 0, 2),
-    (2, 0, 1, 2), (2, 1, 1, 2), (2, 0, 2, 2), (2, 1, 2, 2), (2, 0, 3, 2), (2, 1, 3, 2), (2, 0, 0, 3),
-    (2, 1, 0, 3), (1, 4), (2, 0, 1, 3), (2, 1, 1, 3), (1, 5), (2, 0, 2, 3), (2, 1, 2, 3), (1, 6),
-    (2, 0, 3, 3), (2, 1, 3, 3), (1, 7), (2, 1, 4, 1), (2, 0, 0, 4), (3, 0), (2, 1, 1, 4), (3, 1),
-    (2, 0, 4, 1), (2, 0, 5, 1), (2, 1, 5, 1), (2, 1, 6, 1), (2, 0, 2, 4), (3, 2), (4, 0, 0, 1), (4, 1, 0, 1),
-    (2, 0, 6, 1), (2, 1, 3, 4), (3, 3), (2, 0, 7, 1), (2, 1, 7, 1), (4, 0, 1, 1), (4, 1, 1, 1), (2, 0, 4, 2),
-    (2, 1, 4, 2), (4, 0, 2, 1), (4, 1, 2, 1), (2, 0, 5, 2), (2, 1, 5, 2), (4, 0, 0, 2), (4, 1, 0, 2),
-    (4, 0, 3, 1), (2, 0, 6, 2), (2, 1, 6, 2), (4, 1, 3, 1), (4, 0, 1, 2), (4, 1, 1, 2), (2, 0, 7, 2),
-    (2, 1, 7, 2), (4, 0, 2, 2), (4, 1, 2, 2), (2, 0, 4, 3), (2, 1, 4, 3), (4, 0, 0, 3), (4, 1, 0, 3),
-    (2, 0, 5, 3), (2, 1, 5, 3), (4, 0, 3, 2), (4, 1, 3, 2), (4, 0, 1, 3), (2, 0, 6, 3), (2, 1, 6, 3),
-    (4, 1, 1, 3), (4, 0, 2, 3), (4, 1, 2, 3), (2, 0, 7, 3), (2, 1, 7, 3), (4, 0, 0, 4), (5, 0), (2, 0, 4, 4),
-    (3, 4), (4, 0, 3, 3), (4, 1, 3, 3), (4, 1, 1, 4), (2, 0, 6, 4), (3, 6), (2, 1, 5, 4), (3, 5),
-    (2, 1, 7, 4), (3, 7), (4, 0, 4, 1), (4, 1, 4, 1), (4, 1, 3, 4), (5, 1), (4, 0, 6, 1), (4, 0, 2, 4),
-    (5, 2), (4, 1, 6, 1), (4, 0, 5, 1), (4, 1, 5, 1), (4, 0, 7, 1), (4, 1, 7, 1), (4, 0, 4, 2), (4, 1, 4, 2),
-    (4, 0, 6, 2), (4, 1, 6, 2), (5, 3), (4, 0, 5, 2), (4, 1, 5, 2), (4, 0, 7, 2), (4, 1, 7, 2), (4, 0, 4, 3),
-    (4, 1, 4, 3), (4, 0, 6, 3), (4, 1, 6, 3), (4, 0, 5, 3), (4, 1, 5, 3), (4, 0, 7, 3), (4, 1, 7, 3),
-    (4, 0, 4, 4), (5, 4), (4, 0, 6, 4), (5, 6), (4, 1, 5, 4), (4, 1, 7, 4), (5, 5), (5, 7),
+    (0, 0), (1, 0), (0, 1), (1, 2), (0, 2), (1, 4), (2, 1, 0, 1), (2, 0, 0, 1), (1, 5), (2, 1, 2, 1), (0, 3),
+    (1, 6), (2, 0, 2, 1), (2, 1, 0, 2), (2, 0, 0, 2), (1, 7), (2, 0, 6, 1), (2, 1, 2, 2), (2, 0, 2, 2),
+    (2, 1, 0, 3), (2, 1, 4, 1), (2, 0, 0, 3), (2, 0, 4, 1), (2, 1, 6, 1), (2, 1, 2, 3), (2, 1, 7, 1),
+    (2, 0, 6, 2), (2, 1, 4, 2), (2, 0, 7, 1), (2, 0, 0, 4), (2, 0, 2, 3), (2, 1, 5, 1), (2, 0, 4, 2),
+    (2, 1, 2, 4), (2, 1, 7, 2), (2, 0, 5, 1), (6, 0), (2, 0, 6, 3), (2, 1, 6, 2), (3, 0), (3, 1),
+    (2, 0, 4, 3), (2, 1, 5, 2), (6, 1), (2, 0, 7, 2), (3, 3), (3, 2), (4, 0, 0, 1), (2, 1, 6, 3),
+    (2, 0, 6, 4), (2, 1, 7, 3), (2, 0, 5, 2), (4, 1, 0, 1), (2, 1, 4, 3), (3, 6), (4, 0, 1, 1), (2, 1, 5, 3),
+    (4, 1, 1, 1), (2, 0, 4, 4), (3, 4), (4, 0, 2, 1), (4, 1, 3, 1), (4, 1, 0, 2), (2, 0, 7, 3), (4, 0, 0, 2),
+    (2, 0, 5, 3), (2, 1, 7, 4), (4, 1, 2, 1), (4, 0, 6, 1), (3, 7), (4, 0, 4, 1), (2, 1, 5, 4), (4, 1, 6, 1),
+    (3, 5), (4, 0, 2, 2), (4, 1, 4, 1), (4, 0, 3, 1), (4, 1, 3, 2), (4, 0, 6, 2), (4, 0, 0, 3), (4, 1, 0, 3),
+    (4, 1, 7, 1), (4, 1, 2, 2), (4, 0, 4, 2), (4, 1, 5, 1), (4, 0, 2, 3), (4, 1, 1, 2), (4, 0, 7, 1),
+    (4, 1, 6, 2), (4, 0, 6, 3), (4, 1, 7, 2), (4, 0, 5, 1), (4, 0, 0, 4), (5, 0), (4, 1, 4, 2), (4, 1, 2, 3),
+    (4, 0, 4, 3), (4, 1, 5, 2), (4, 0, 1, 2), (4, 0, 2, 4), (5, 2), (4, 0, 3, 2), (4, 1, 1, 3), (4, 1, 3, 3),
+    (4, 0, 6, 4), (4, 1, 6, 3), (5, 6), (4, 0, 7, 2), (4, 1, 7, 3), (4, 0, 5, 2), (4, 1, 4, 3), (4, 0, 4, 4),
+    (5, 4), (4, 1, 5, 3), (4, 0, 3, 3), (4, 1, 7, 4), (4, 1, 3, 4), (4, 0, 1, 3), (5, 3), (4, 1, 1, 4),
+    (4, 0, 7, 3), (5, 1), (4, 0, 5, 3), (5, 7), (4, 1, 5, 4), (5, 5),
 )
 
 
@@ -52,7 +51,7 @@
 
 
 def kernel(nh, lam, w, mask, out, q_buf, a_buf, w_buf, p_buf, e_buf, r_buf, x_buf, fx_buf, t_buf, s_buf,
-           lam_s, lam_r, lam_l, w_s, w_r, w_l, ag_s, ag_r, rs_s, rs_r, x_s, x_r, t_s, t_r):
+           lam_s, lam_r, lam_l, w_s, w_r, w_l, ag_s, ag_r, xg_s, xg_r, rs_s, rs_r, x_s, x_r, t_s, t_r):
     nst = 2 * nh
     ij = lam.shape[2]
     half = ij // 2
@@ -130,13 +129,13 @@
         a_buf[2 * i + x_lo, z] = block[half:]
 
     def ag_hops(d, s):
-        return NZ // 2 if d == s % 2 else NZ // 2 - 1
+        return NZ // 2 if d == (s // 2 if s < 2 * NF else s) % 2 else NZ // 2 - 1
 
     def ag_from(d, back):
         return (z + NZ - back) % NZ if d == 0 else (z + back) % NZ
 
     def ag_copy(d, s, k, back):
-        block = a_buf.at[s, ag_from(d, back)]
+        block = a_buf.at[s + x_hi if s < 2 * NF else s, ag_from(d, back)]
         return remote(block, block, ag_s.at[d, s, k - 1], ag_r.at[d, s, k - 1], z_to[d])
 
     def ag_start(d, s, k):
@@ -144,6 +143,10 @@
 
     def ag_wait(d, s, k):
         ag_copy(d, s, k, k).wait_recv()
+
+    def xg_copy(d, s, k, side):
+        block = a_buf.at[s + side, ag_from(d, k)]
+        return remote(block, block, xg_s.at[d, s // 2, k - 1], xg_r.at[d, s // 2, k - 1], quads[1][0])
 
     def rs_hops(d, s):
         return NY // 2 if d == s % 2 else NY // 2 - 1
@@ -171,9 +174,12 @@
     def t_copy(i):
         return remote(t_buf.at[i], s_buf.at[i], t_s.at[i], t_r.at[i], sibling)
 
+    weights = set()
+
     def matmul(s):
         i = s // 2
-        if s % 2 == 0:
+        if i not in weights:
+            weights.add(i)
             w_local(i).wait()
             w_send(i).wait_recv()
         block = jnp.concatenate([a_buf[s, k] for k in range(NZ)], axis=1)
@@ -198,6 +204,13 @@
         ag_wait(d, s, k)
         if k < ag_hops(d, s):
             ag_start(d, s, k + 1)
+        if s < 2 * NF:
+            xg_copy(d, s, k, x_hi).start()
+
+    def swapped(i):
+        for d in range(2):
+            for k in range(1, ag_hops(d, 2 * i) + 1):
+                xg_copy(d, 2 * i, k, 1 - x_hi).wait_recv()
 
     def gather_first(s):
         for d in range(2):
@@ -211,7 +224,7 @@
     def sum_step(d, s, k):
         rs_arrive(d, s, rs_hops(d, s) - k)
 
-    steps = (prep, gather_first, gather_step, multiply, sum_step, final)
+    steps = (prep, gather_first, gather_step, multiply, sum_step, final, swapped)
     for kind, *which in ORDER:
         steps[kind](*which)
 
@@ -227,8 +240,10 @@
         t_copy(i).wait_send()
     for s in range(nst):
         for d in range(2):
-            for k in range(1, ag_hops(d, s) + 1):
+            for k in range(1, ag_hops(d, s) + 1 if s >= 2 * NF or s % 2 == 0 else 1):
                 ag_copy(d, s, k, k - 1).wait_send()
+                if s < 2 * NF:
+                    xg_copy(d, s, k, x_hi).wait_send()
             for m in range(1, rs_hops(d, s) + 1):
                 rs_copy(d, s, m).wait_send()
 
@@ -262,6 +277,7 @@
             dma((3, nh)), dma((3, nh)), dma((nh,)),
             dma((nh,)), dma((nh,)), dma((nh,)),
             dma((2, nst, 4)), dma((2, nst, 4)),
+            dma((2, NF, 4)), dma((2, NF, 4)),
             dma((2, nst, 4)), dma((2, nst, 4)),
             dma((nh,)), dma((nh,)),
             dma((nh,)), dma((nh,)),

time: 75.1 us -> 70.3 us (0.936)
  Pallas kernels: 73.3 us -> 68.5 us
    pallas_call x1, Pallas kernels: 73.3 us -> 68.5 us  [per_device(): pl.pallas_call(functools.partial(kernel, nh), out_shape=jax.ShapeDtypeStr...]
where the time goes in v4:
time: 70.3 us; the launch traced here: 70.1 us
  Pallas kernels  68.5 us (97%)
  local copies, waits for them, and re-layouts  1.54 us (2%)
    pallas_call x1, Pallas kernels, per_device(): pl.pallas_call(functools.partial(kernel, nh), out_shape=jax.ShapeDtypeStr...  68.5 us
    unnamed x1, local copies, waits for them, and re-layouts  1.54 us

profile of v4, /device:TPU:1, one launch (start us, length us, event | category | flops | bytes accessed | tf_op | source)
XLA Modules:
  0.0 70.1 jit_solution(8008954170925355083)
XLA Ops:
  0.0 68.5 %shard_map.37 = bf16[8,24,256]{2,1,0:T(8,128)(2,1)} custom-call(bf16[8,32,384]{2,1,0:T(8,128)(2,1)} %bitcast.1, bf16[8,1024,256]{2,1,0:T(8,128)(2,1)} %w.1, s32[8,32]{1,0:T(8,128)} %mask.1), custom_call_target="tpu_custom_call" | custom-call | tf_op jit(solution)/shard_map/pallas_call | solution.py:261
  68.5 1.5 %copy.5 = bf16[8,24,256]{2,1,0:T(8,128)(2,1)} copy(bf16[8,24,256]{2,1,0:T(8,128)(2,1)} %shard_map.37) | data formatting | bytes 196608

commit v5 on v4

--- a/solution.py
+++ b/solution.py
@@ -14,7 +14,7 @@
 NQ = 4
 F32 = jnp.float32
 I16 = jnp.int16
-SCALE_ROWS = 16
+SCALE_ROWS = 8
 
 ORDER = (
     (0, 0), (1, 0), (0, 1), (1, 2), (0, 2), (1, 4), (2, 1, 0, 1), (2, 0, 0, 1), (1, 5), (2, 1, 2, 1), (0, 3),

time: 70.3 us -> 69.4 us (0.987)
  Pallas kernels: 68.5 us -> 67.7 us
    pallas_call x1, Pallas kernels: 68.5 us -> 67.7 us  [per_device(): pl.pallas_call(functools.partial(kernel, nh), out_shape=jax.ShapeDtypeStr...]
where the time goes in v5:
time: 69.4 us; the launch traced here: 69.2 us
  Pallas kernels  67.7 us (98%)
  local copies, waits for them, and re-layouts  1.54 us (2%)
    pallas_call x1, Pallas kernels, per_device(): pl.pallas_call(functools.partial(kernel, nh), out_shape=jax.ShapeDtypeStr...  67.7 us
    unnamed x1, local copies, waits for them, and re-layouts  1.54 us

profile of v5, /device:TPU:1, one launch (start us, length us, event | category | flops | bytes accessed | tf_op | source)
XLA Modules:
  0.0 69.2 jit_solution(14068140201127688985)
XLA Ops:
  0.0 67.7 %shard_map.37 = bf16[8,24,256]{2,1,0:T(8,128)(2,1)} custom-call(bf16[8,32,384]{2,1,0:T(8,128)(2,1)} %bitcast.1, bf16[8,1024,256]{2,1,0:T(8,128)(2,1)} %w.1, s32[8,32]{1,0:T(8,128)} %mask.1), custom_call_target="tpu_custom_call" | custom-call | tf_op jit(solution)/shard_map/pallas_call | solution.py:261
  67.7 1.5 %copy.5 = bf16[8,24,256]{2,1,0:T(8,128)(2,1)} copy(bf16[8,24,256]{2,1,0:T(8,128)(2,1)} %shard_map.37) | data formatting | bytes 196608
